TPU v7x, 32 devices: a whole 2x2x4 slice. The times are simulated.
32 devices in a mesh: space: 8 (over z, x), member: 4 (over y, core).
Axes of the slice: x: 2, y: 2, z: 4, core: 2. Of those that a mesh axis runs over, the one named last changes fastest.
Arguments:
- prediction_maps: bfloat16 [4, 72, 16, 1440], P('member', None, 'space'), may hold values from -6 to 6
- truth_analysis: float32 [72, 23040], P(None, ('space', 'member')), may hold values from -6 to 6
- reciprocal_spread: float32 [72], replicated, may hold values from 0.3 to 3
- deconv_inputs: bfloat16 [4, 72, 16, 1440], P('member', None, 'space'), may hold values from -6 to 6
- filter_tensor: bfloat16 [5, 5, 72, 72], replicated, may hold values from -0.125 to 0.125
Outputs:
- grad_hidden: bfloat16 [4, 72, 16, 1440], P('member', None, 'space')
- grad_kernel: float32 [5, 5, 72, 72], replicated
All inputs are finite; a program needn't handle non-finite values.
Results may differ from a plain program's by a relative error of at most 0.018.
Values may be sent and summed in bfloat16 or wider, within the bound.
No kernel may reach another device: no remote copies, remote signals or barrier semaphores. Data moves between devices by JAX's collectives and lax.ppermute only.
A program may use at most 64 MiB of HBM per device.

v0:
```python
import jax
import jax.numpy as jnp
from jax import lax
from jax.sharding import PartitionSpec as P

smoothing = 1.0


def extended(x, sides, width):
    for axis, dim in sides:
        size, length = (lax.axis_size(axis), x.shape[dim])
        up = [(i, (i + 1) % size) for i in range(size - 1)]
        down = [(j, i) for i, j in up]
        last = lax.slice_in_dim(x, length - width, length, axis=dim)
        first = lax.slice_in_dim(x, 0, width, axis=dim)
        before = lax.ppermute(last, axis, up)
        after = lax.ppermute(first, axis, down)
        x = jnp.concatenate([before, x, after], axis=dim)
    return x


def area_weights(rows_total):
    index = jnp.arange(rows_total, dtype=jnp.float32)
    latitude = (index + 0.5) * (jnp.pi / rows_total) - jnp.pi / 2
    cosine = jnp.cos(latitude)
    return cosine / jnp.mean(cosine)


def direct_term(own, target, scale):
    offset = scale * (own - target[None])
    radius = jnp.sqrt(jnp.sum(offset * offset, axis=1, keepdims=True) + smoothing)
    return scale * offset / radius


def pair_sums(scaled_own, scaled_other):
    own_sq = jnp.sum(scaled_own * scaled_own, axis=1)
    other_sq = jnp.sum(scaled_other * scaled_other, axis=1)
    inner = jnp.einsum("mcp,ncp->mnp", scaled_own, scaled_other, precision=lax.Precision.HIGHEST)
    spread_sq = own_sq[:, None, :] + other_sq[None, :, :] - 2.0 * inner + smoothing
    inverse = 1.0 / jnp.sqrt(spread_sq)
    total_weight = jnp.sum(inverse, axis=1)
    mixture = jnp.einsum("mnp,ncp->mcp", inverse, scaled_other, precision=lax.Precision.HIGHEST)
    return (total_weight, mixture)


def body(prediction_maps, truth_analysis, reciprocal_spread, deconv_inputs, filter_tensor):
    quantity_indices = prediction_maps.shape[1]
    parallel_section = prediction_maps.shape[2]
    meridian_extent = prediction_maps.shape[3]
    ksize = filter_tensor.shape[0]
    members = lax.axis_size("member")
    rows_total = parallel_section * lax.axis_size("space")
    pixel_count = parallel_section * meridian_extent
    weights = lax.dynamic_slice_in_dim(
        area_weights(rows_total), lax.axis_index("space") * parallel_section, parallel_section
    )
    scale = reciprocal_spread[None, :, None]
    prediction_vector = prediction_maps.reshape(1, quantity_indices, pixel_count)
    whole_obs = lax.all_gather(truth_analysis, "member", axis=1, tiled=True)
    own = prediction_vector.astype(jnp.float32)
    direct = direct_term(own, whole_obs, scale)
    scaled_own = scale * own
    piece = lax.all_gather(prediction_maps, "member", axis=0, tiled=True)
    other = scale * piece.astype(jnp.float32).reshape(piece.shape[0], quantity_indices, pixel_count)
    weight_part, mix_part = pair_sums(scaled_own, other)
    paired = scale * (scaled_own * weight_part[:, None, :] - mix_part)
    terms = (direct - paired / members).reshape(quantity_indices, parallel_section, meridian_extent)
    grad_out = (terms * weights[None, :, None]).astype(jnp.bfloat16)
    padded = extended(grad_out, (("space", 1),), 2)
    wrapped = jnp.concatenate([padded[:, :, -2:], padded, padded[:, :, :2]], axis=2)
    flat_hidden = deconv_inputs[0].reshape(quantity_indices, pixel_count)
    back = jnp.zeros((quantity_indices, pixel_count), jnp.float32)
    pieces = []
    for row_shift in range(ksize):
        band = wrapped[:, row_shift : row_shift + parallel_section, :]
        stacked = jnp.stack(
            [band[:, :, col_shift : col_shift + meridian_extent] for col_shift in range(ksize)]
        ).reshape(ksize * quantity_indices, pixel_count)
        row_filter = jnp.transpose(filter_tensor[row_shift], (1, 0, 2)).reshape(
            quantity_indices, ksize * quantity_indices
        )
        back = back + jnp.dot(row_filter, stacked, preferred_element_type=jnp.float32)
        product = lax.dot_general(
            flat_hidden, stacked, (((1,), (1,)), ((), ())), preferred_element_type=jnp.float32
        )
        pieces.append(
            jnp.transpose(product.reshape(quantity_indices, ksize, quantity_indices), (1, 0, 2))
        )
    partial_sum = jnp.stack(pieces)
    grad_hidden = back.astype(jnp.bfloat16).reshape(
        1, quantity_indices, parallel_section, meridian_extent
    )
    kernel_total = lax.psum(partial_sum, ("space", "member"))
    norm_factor = 1.0 / jnp.sqrt(jnp.float32(members * rows_total * meridian_extent))
    return (grad_hidden, kernel_total * norm_factor)


def solution(mesh):
    return jax.shard_map(
        body,
        mesh=mesh,
        in_specs=(
            P("member", None, "space", None),
            P(None, ("space", "member")),
            P(),
            P("member", None, "space", None),
            P(),
        ),
        out_specs=(P("member", None, "space", None), P()),
        check_vma=False,
    )
```

profile of v0, /device:TPU:0, one launch (start us, length us, event | category | flops | bytes accessed | tf_op | source)
XLA Modules:
  0.0 303.7 jit_solution(18112935933690532214)
XLA Ops:
  7.2 1.9 copy.52
  9.2 1.3 reshape.255
  10.8 10.8 %all-gather = f32[4,720,72]{1,2,0:T(8,128)S(1)} all-gather(f32[1,720,72]{1,2,0:T(8,128)S(1)} %bitcast.231), channel_id=1, replica_groups=mesh['space'=8,'member'=4] {'member'}, dimensions={0}, use_global_device_ids=true | all-gather | bytes 1036800 | tf_op jit(solution)/shard_map/all_gather | solution.py:59
  21.9 0.6 reshape.258
  22.5 0.8 fusion.35
  24.3 1.2 multiply_reduce_fusion.4
  25.4 8.2 %all-gather.3.cloned.1.call-done = bf16[4,72,2,1440]{3,1,2,0:T(8,128)(2,1)} async-done(((bf16[1,72,2,1440]{3,1,2,0:T(8,128)(2,1)}), bf16[4,72,2,1440]{3,1,2,0:T(8,128)(2,1)}) %all-gather.3.cloned.1.call-update) | async-done | bytes 1658896 | tf_op jit(solution)/shard_map/all_gather | solution.py:63
  33.6 4.6 %copy.53 = f32[4,72,2,1440]{3,2,1,0:T(2,128)} copy(bf16[4,72,2,1440]{3,1,2,0:T(8,128)(2,1)} %all-gather.3.cloned.1.call-done) | data formatting | bytes 4976640 | tf_op jit(solution)/shard_map/convert_element_type | solution.py:64
  38.2 4.7 %reshape.235 = f32[4,72,2880]{2,1,0:T(8,128)S(1)} reshape(f32[4,72,2,1440]{3,2,1,0:T(2,128)} %copy.53) | data formatting | bytes 6635520 | tf_op jit(solution)/shard_map/reshape | solution.py:64
  42.9 2.1 multiply_reduce_fusion
  45.2 1.6 multiply_reduce_fusion.2
  47.4 0.6 copy-done.5
  48.9 0.9 reshape.237
  50.3 3.4 %collective-permute-start = (bf16[72,2,1440]{2,1,0:T(2,128)(2,1)S(1)}, bf16[72,2,1440]{2,1,0:T(2,128)(2,1)S(1)}, u32[]{:S(2)}, u32[]{:S(2)}) collective-permute-start(bf16[72,2,1440]{2,1,0:T(2,128)(2,1)S(1)} %multiply_convert_fusion.1), channel_id=1, source_target_pairs={{0,4},{4,8},{8,12},{12,16},{16,20},{20,24},{24,28},{1,5},{5,9},{9,... | collective-permute-start | bytes 1244168 | tf_op jit(solution)/shard_map/ppermute | solution.py:16
  53.7 1.5 collective-permute-start.1
  55.6 0.7 copy.54
  56.3 0.8 copy.55
  57.1 0.7 copy.56
  57.8 0.7 copy.57
  58.5 0.7 copy.58
  59.3 0.9 reshape.242
  60.2 12.7 %collective-permute-done = bf16[72,2,1440]{2,1,0:T(2,128)(2,1)S(1)} collective-permute-done((bf16[72,2,1440]{2,1,0:T(2,128)(2,1)S(1)}, bf16[72,2,1440]{2,1,0:T(2,128)(2,1)S(1)}, u32[]{:S(2)}, u32[]{:S(2)}) %collective-permute-start) | collective-permute-done | bytes 414752 | tf_op jit(solution)/shard_map/ppermute | solution.py:16
  72.9 7.4 %fusion.2 = (bf16[72,6,1442]{2,1,0:T(8,128)(2,1)S(1)}, bf16[72,6,1442]{2,1,0:T(8,128)(2,1)S(1)}) fusion(bf16[72,2,1440]{2,1,0:T(2,128)(2,1)} %collective-permute-done.1, bf16[72,2,1440]{2,1,0:T(2,128)(2,1)S(1)} %multiply_convert_fusion.1, bf16[72,2,1440]{2,1,0:T(2,128)(2,1)S(1)} %collective-permute-done), kind=kLoop, calls=%fused_computation.10 | loop fusion | flops 14950656 | bytes 3735936 | tf_op jit(solution)/shard_map/concatenate | solution.py:70
  80.3 1.6 fusion.12
  82.0 5.2 %fusion.11 = (bf16[5,72,2,1440]{3,2,1,0:T(2,128)(2,1)S(1)}, bf16[5,72,2,1440]{3,2,1,0:T(2,128)(2,1)S(1)}, bf16[5,72,2,1440]{3,2,1,0:T(2,128)(2,1)S(1)}, bf16[5,7...) fusion(bf16[5,72,2,1440]{3,2,1,0:T(2,128)(2,1)S(1)} %get-tuple-element.25, ...), kind=kLoop, calls=%fused_computation.38 | loop fusion | bytes 4423680
  87.6 3.8 %bitcast_dynamic-update-slice_fusion = (bf16[5,72,2,1440]{3,2,1,0:T(2,128)(2,1)S(1)}, bf16[5,72,2,1440]{3,2,1,0:T(2,128)(2,1)S(1)}, bf16[5,72,2,1440]{3,2,1,0:T(2,128)(2,1)S(1)}, bf16[5,72,2,1440]{3,2,1,0:T(2,128)(2,1)S(1)}) fusion(bf16[5,72,2,1440]{3,2,1,0:T(2,128)(2,1)S(1)} %get-tuple-element.20, bf16[72,2,1440]{2,1,0:T(2,128)(2,1)} %collective-permute-done.1, ...), kind=kLoop, calls=%fused_computation.79 | loop fusion | flops 1658880 | bytes 3068928
  91.3 5.2 %fusion.10 = (bf16[5,72,2,1440]{3,2,1,0:T(2,128)(2,1)S(1)}, bf16[5,72,2,1440]{3,2,1,0:T(2,128)(2,1)S(1)}, bf16[5,72,2,1440]{3,2,1,0:T(2,128)(2,1)S(1)}, bf16[5,7...) fusion(bf16[5,72,2,1440]{3,2,1,0:T(2,128)(2,1)S(1)} %get-tuple-element.39, ...), kind=kLoop, calls=%fused_computation.36 | loop fusion | bytes 4423680
  96.5 5.4 %fusion.9 = (bf16[5,72,2,1440]{3,2,1,0:T(2,128)(2,1)S(1)}, bf16[5,72,2,1440]{3,2,1,0:T(2,128)(2,1)S(1)}, bf16[5,72,2,1440]{3,2,1,0:T(2,128)(2,1)S(1)}, bf16[5,72...) fusion(bf16[5,72,2,1440]{3,2,1,0:T(2,128)(2,1)S(1)} %get-tuple-element.15, ...), kind=kLoop, calls=%fused_computation.34 | loop fusion | bytes 4423680 | tf_op jit(solution)/shard_map/stack | solution.py:76
  101.9 1.4 copy-done.11
  103.2 1.4 copy-done.12
  104.6 1.4 copy-done.13
  106.0 1.4 copy-done.14
  107.5 1.4 copy-done.15
  108.8 5.4 %reshape.238 = bf16[360,2880]{1,0:T(8,128)(2,1)S(1)} reshape(bf16[5,72,2,1440]{3,2,1,0:T(2,128)(2,1)} %copy-done.15) | data formatting | bytes 4147200 | tf_op jit(solution)/shard_map/reshape | solution.py:78
  114.2 0.8 convolution_bitcast_fusion.4
  115.0 0.8 copy.59
  115.8 0.9 constant_dynamic-update-slice_fusion.4
  116.7 6.3 %reshape.240 = bf16[360,2880]{1,0:T(8,128)(2,1)} reshape(bf16[5,72,2,1440]{3,2,1,0:T(2,128)(2,1)} %copy-done.14) | data formatting | bytes 4147200 | tf_op jit(solution)/shard_map/reshape | solution.py:78
  123.0 3.0 convolution_bitcast_fusion.3
  126.0 1.7 copy.60
  127.7 6.3 %reshape.243 = bf16[360,2880]{1,0:T(8,128)(2,1)} reshape(bf16[5,72,2,1440]{3,2,1,0:T(2,128)(2,1)} %copy-done.13) | data formatting | bytes 4147200 | tf_op jit(solution)/shard_map/reshape | solution.py:78
  134.0 3.0 convolution_bitcast_fusion.2
  137.0 1.7 copy.61
  138.7 6.2 %reshape.245 = bf16[360,2880]{1,0:T(8,128)(2,1)} reshape(bf16[5,72,2,1440]{3,2,1,0:T(2,128)(2,1)} %copy-done.12) | data formatting | bytes 4147200 | tf_op jit(solution)/shard_map/reshape | solution.py:78
  144.9 3.0 convolution_bitcast_fusion.1
  148.0 1.7 copy.62
  149.7 6.2 %reshape.247 = bf16[360,2880]{1,0:T(8,128)(2,1)} reshape(bf16[5,72,2,1440]{3,2,1,0:T(2,128)(2,1)} %copy-done.11) | data formatting | bytes 4147200 | tf_op jit(solution)/shard_map/reshape | solution.py:78
  155.9 3.0 convolution_bitcast_fusion
  158.9 1.0 copy.63
  160.0 0.9 constant_dynamic-update-slice_fusion.3
  160.9 0.9 constant_dynamic-update-slice_fusion.2
  161.9 0.9 constant_dynamic-update-slice_fusion.1
  162.8 0.9 copy-done.16
  163.8 0.5 fusion.38
  164.4 1.0 copy-done
  165.4 0.5 convolution_add_fusion.3
  166.2 0.5 convolution_add_fusion.2
  166.7 0.9 copy-done.2
  167.6 0.5 convolution_add_fusion.1
  168.5 0.5 fusion.1
  169.0 1.3 reshape.249
  170.3 124.0 %all-reduce.2.cloned.1.call-done = f32[5,5,72,72]{2,3,1,0:T(8,128)} async-done(((f32[5,5,72,72]{2,3,1,0:T(8,128)}), f32[5,5,72,72]{2,3,1,0:T(8,128)}) %all-reduce.2.cloned.1.call-update) | async-done | bytes 518416 | tf_op jit(solution)/shard_map/psum | solution.py:93
  294.3 1.3 broadcast_multiply_fusion
  295.6 1.2 copy.64
  (63 shorter events, 4.3 us)
Async XLA Ops:
  7.2 3.3 %copy-start.10 = (bf16[1,72,2,1440]{3,2,1,0:T(2,128)(2,1)S(1)}, bf16[1,72,2,1440]{3,2,1,0:T(2,128)(2,1)}, u32[]{:S(2)}) copy-start(bf16[1,72,2,1440]{3,2,1,0:T(2,128)(2,1)} %param.5) | copy-start | bytes 1244164
  7.2 3.6 %copy-start.24 = (f32[72,720]{1,0:T(8,128)S(1)}, f32[72,720]{1,0:T(8,128)}, u32[]{:S(2)}) copy-start(f32[72,720]{1,0:T(8,128)} %param.6) | copy-start | bytes 622084
  7.2 26.4 %all-gather.3.cloned.1.call-start = ((), (), s32[]{:S(2)}) async-start(), calls=%async_computation | async-start | bytes 2211840 | tf_op jit(solution)/shard_map/all_gather | solution.py:63
  9.1 285.2 %all-reduce.2.cloned.1.call-start = ((), (), s32[]{:S(2)}) async-start(), calls=%async_computation.1 | async-start | bytes 1843200 | tf_op jit(solution)/shard_map/psum | solution.py:93
  10.5 13.8 %copy-start.6 = (f32[72,2880]{1,0:T(8,128)}, f32[72,2880]{1,0:T(8,128)S(1)}, u32[]{:S(2)}) copy-start(f32[72,2880]{1,0:T(8,128)S(1)} %reshape.255) | copy-start | bytes 2488324
  10.8 13.3 %copy-start.4 = (f32[1,72,2880]{2,1,0:T(8,128)}, f32[1,72,2880]{2,1,0:T(8,128)S(1)}, u32[]{:S(2)}) copy-start(f32[1,72,2880]{2,1,0:T(8,128)S(1)} %reshape.256) | copy-start | bytes 2488324
  10.8 13.3 %copy-start.25 = (f32[72]{0:T(128)S(1)}, f32[72]{0:T(128)}, u32[]{:S(2)}) copy-start(f32[72]{0:T(128)} %param.7) | copy-start | bytes 868
  22.5 11.1 %copy-start.8 = (f32[2880,72]{0,1:T(8,128)}, f32[2880,72]{0,1:T(8,128)S(1)}, u32[]{:S(2)}) copy-start(f32[2880,72]{0,1:T(8,128)S(1)} %reshape.258) | copy-start | bytes 2488324
  46.9 1.2 copy-start.5
  46.9 1.4 copy-start.7
  46.9 1.6 copy-start.9
  48.9 6.2 %copy-start.18 = (bf16[1,72,2,1440]{3,2,1,0:T(2,128)(2,1)S(1)}, bf16[1,72,2,1440]{3,2,1,0:T(2,128)(2,1)}, u32[]{:S(2)}) copy-start(bf16[1,72,2,1440]{3,2,1,0:T(2,128)(2,1)} %param.8) | copy-start | bytes 1244164
  48.9 6.6 %copy-start.17 = (bf16[5,5,72,72]{3,2,1,0:T(8,128)(2,1)S(1)}, bf16[5,5,72,72]{3,2,1,0:T(8,128)(2,1)}, u32[]{:S(2)}) copy-start(bf16[5,5,72,72]{3,2,1,0:T(8,128)(2,1)} %param.9) | copy-start | bytes 777604
  50.3 22.7 %collective-permute-start = (bf16[72,2,1440]{2,1,0:T(2,128)(2,1)S(1)}, bf16[72,2,1440]{2,1,0:T(2,128)(2,1)S(1)}, u32[]{:S(2)}, u32[]{:S(2)}) collective-permute-start(bf16[72,2,1440]{2,1,0:T(2,128)(2,1)S(1)} %multiply_convert_fusion.1), channel_id=1, source_target_pairs={{0,4},{4,8},{8,12},{12,16},{16,20},{20,24},{24,28},{1,5},{5,9},{9,... | collective-permute-start | bytes 1244168 | tf_op jit(solution)/shard_map/ppermute | solution.py:16
  53.7 19.3 %collective-permute-start.1 = (bf16[72,2,1440]{2,1,0:T(2,128)(2,1)S(1)}, bf16[72,2,1440]{2,1,0:T(2,128)(2,1)}, u32[]{:S(2)}, u32[]{:S(2)}) collective-permute-start(bf16[72,2,1440]{2,1,0:T(2,128)(2,1)S(1)} %multiply_convert_fusion.1), channel_id=1, source_target_pairs={{4,0},{8,4},{12,8},{16,12},{20,16},{24,20},{28,24},{5,1},{9,5},{13... | collective-permute-start | bytes 1244168 | tf_op jit(solution)/shard_map/ppermute | solution.py:17
  101.9 1.4 copy-start.11
  103.2 1.4 copy-start.12
  104.6 1.4 copy-start.13
  106.0 1.4 copy-start.14
  107.5 1.4 copy-start.15
  158.9 4.9 %copy-start.23 = (bf16[72,5,72]{0,2,1:T(8,128)(2,1)S(1)}, bf16[72,5,72]{0,2,1:T(8,128)(2,1)}, u32[]{:S(2)}) copy-start(bf16[72,5,72]{0,2,1:T(8,128)(2,1)} %copy.54) | copy-start | bytes 155524
  162.8 1.6 copy-start.22
  162.8 0.9 copy-start.16
  163.8 1.6 copy-start
  164.4 1.8 copy-start.1
  164.4 1.8 copy-start.21
  165.9 1.7 copy-start.2
  165.9 1.7 copy-start.20
  166.7 1.8 copy-start.3
  166.7 1.8 copy-start.19
Sparse Core Ops, SparseCore 0:
  10.1 23.4 all-gather.2
  163.9 130.3 all-reduce.1
where the time goes:
time: 305 us; the launch traced here: 304 us
  waiting for transfers between devices  145 us (48%)
  local copies, waits for them, and re-layouts  92.3 us (30%)
  other arithmetic  20 us (7%)
  matrix products  15.6 us (5%)
  between operations  15.2 us (5%)
  blocking collectives  10.8 us (4%)
  starting transfers between devices  4.95 us (2%)
    psum x1, waiting for transfers between devices, body(): kernel_total = lax.psum(partial_sum, ('space', 'member'))  124 us
    unnamed x62, local copies, waits for them, and re-layouts  30.9 us
    reshape x5, local copies, waits for them, and re-layouts, body(): stacked = jnp.stack([band[:, :, col_shift:col_shift + meridian_extent] fo...  30.4 us
    dot_general x5, matrix products, body(): lax.dot_general(flat_hidden, stacked, (((1,), (1,)), ((), ())), preferred...  12.9 us
    ppermute x1, waiting for transfers between devices, extended(): before = lax.ppermute(last, axis, up)  12.7 us
    all_gather x1, blocking collectives, body(): whole_obs = lax.all_gather(truth_analysis, 'member', axis=1, tiled=True)  10.8 us
    all_gather x1, waiting for transfers between devices, body(): piece = lax.all_gather(prediction_maps, 'member', axis=0, tiled=True)  8.17 us
    concatenate x1, other arithmetic, body(): jnp.concatenate([padded[:, :, -2:], padded, padded[:, :, :2]], axis=2)  7.37 us
  transfers between devices with their start and end apart: 4, of which 3 were waited for; matrix products, arithmetic and copies ran while one was open for 5% of the time, Pallas kernels for 0%

commit v1 on v0

--- a/solution.py
+++ b/solution.py
@@ -90,7 +90,7 @@
     grad_hidden = back.astype(jnp.bfloat16).reshape(
         1, quantity_indices, parallel_section, meridian_extent
     )
-    kernel_total = lax.psum(partial_sum, ("space", "member"))
+    kernel_total = jax.lax.psum(jax.lax.psum(partial_sum, "member"), axis_name="space")
     norm_factor = 1.0 / jnp.sqrt(jnp.float32(members * rows_total * meridian_extent))
     return (grad_hidden, kernel_total * norm_factor)
 

time: 305 us -> 284 us (0.931)
  waiting for transfers between devices: 145 us -> 128 us
    psum x1 -> x2, waiting for transfers between devices: 124 us -> 109 us  [the longest x1 77.4 us: body(): jax.lax.psum(jax.lax.psum(partial_sum, 'member'), axis_name='space')]
    dot_general x5, matrix products: 12.9 us -> 9.61 us  [body(): lax.dot_general(flat_hidden, stacked, (((1,), (1,)), ((), ())), preferred...]
    unnamed x62 -> x60, local copies, waits for them, and re-layouts: 30.9 us -> 30.5 us
  transfers between devices with their start and end apart: 4 -> 5, of which waited for: 3 -> 4; matrix products, arithmetic and copies ran while one was open for 5% -> 6% of each run, Pallas kernels for 0% -> 0%
where the time goes in v1:
time: 284 us; the launch traced here: 283 us
  waiting for transfers between devices  128 us (45%)
  local copies, waits for them, and re-layouts  92.3 us (32%)
  other arithmetic  17.6 us (6%)
  between operations  14.9 us (5%)
  matrix products  14.1 us (5%)
  blocking collectives  10.8 us (4%)
  starting transfers between devices  5.26 us (2%)
    psum x1, waiting for transfers between devices, body(): jax.lax.psum(jax.lax.psum(partial_sum, 'member'), axis_name='space')  77.4 us
    psum x1, waiting for transfers between devices, body(): jax.lax.psum(partial_sum, 'member')  31.9 us
    unnamed x60, local copies, waits for them, and re-layouts  30.5 us
    reshape x5, local copies, waits for them, and re-layouts, body(): stacked = jnp.stack([band[:, :, col_shift:col_shift + meridian_extent] fo...  28.6 us
    all_gather x1, blocking collectives, body(): whole_obs = lax.all_gather(truth_analysis, 'member', axis=1, tiled=True)  10.8 us
    ppermute x1, waiting for transfers between devices, extended(): before = lax.ppermute(last, axis, up)  10.6 us
    dot_general x5, matrix products, body(): lax.dot_general(flat_hidden, stacked, (((1,), (1,)), ((), ())), preferred...  9.61 us
    all_gather x1, waiting for transfers between devices, body(): piece = lax.all_gather(prediction_maps, 'member', axis=0, tiled=True)  8.17 us
  transfers between devices with their start and end apart: 5, of which 4 were waited for; matrix products, arithmetic and copies ran while one was open for 6% of the time, Pallas kernels for 0%

profile of v1, /device:TPU:0, one launch (start us, length us, event | category | flops | bytes accessed | tf_op | source)
XLA Modules:
  0.0 282.9 jit_solution(16354958120581019397)
XLA Ops:
  7.2 1.9 copy.52
  9.2 1.3 reshape.255
  10.8 10.8 %all-gather = f32[4,720,72]{1,2,0:T(8,128)S(1)} all-gather(f32[1,720,72]{1,2,0:T(8,128)S(1)} %bitcast.231), channel_id=1, replica_groups=mesh['space'=8,'member'=4] {'member'}, dimensions={0}, use_global_device_ids=true | all-gather | bytes 1036800 | tf_op jit(solution)/shard_map/all_gather | solution.py:59
  21.9 0.6 reshape.258
  22.5 0.8 fusion.35
  24.3 1.2 multiply_reduce_fusion.4
  25.4 8.2 %all-gather.3.cloned.1.call-done = bf16[4,72,2,1440]{3,1,2,0:T(8,128)(2,1)} async-done(((bf16[1,72,2,1440]{3,1,2,0:T(8,128)(2,1)}), bf16[4,72,2,1440]{3,1,2,0:T(8,128)(2,1)}) %all-gather.3.cloned.1.call-update) | async-done | bytes 1658896 | tf_op jit(solution)/shard_map/all_gather | solution.py:63
  33.6 4.6 %copy.53 = f32[4,72,2,1440]{3,2,1,0:T(2,128)} copy(bf16[4,72,2,1440]{3,1,2,0:T(8,128)(2,1)} %all-gather.3.cloned.1.call-done) | data formatting | bytes 4976640 | tf_op jit(solution)/shard_map/convert_element_type | solution.py:64
  38.2 4.7 %reshape.235 = f32[4,72,2880]{2,1,0:T(8,128)S(1)} reshape(f32[4,72,2,1440]{3,2,1,0:T(2,128)} %copy.53) | data formatting | bytes 6635520 | tf_op jit(solution)/shard_map/reshape | solution.py:64
  42.9 2.1 multiply_reduce_fusion
  45.2 1.6 multiply_reduce_fusion.2
  47.4 0.6 copy-done.6
  48.9 0.9 reshape.237
  50.3 3.4 %collective-permute-start = (bf16[72,2,1440]{2,1,0:T(2,128)(2,1)S(1)}, bf16[72,2,1440]{2,1,0:T(2,128)(2,1)S(1)}, u32[]{:S(2)}, u32[]{:S(2)}) collective-permute-start(bf16[72,2,1440]{2,1,0:T(2,128)(2,1)S(1)} %multiply_convert_fusion.1), channel_id=1, source_target_pairs={{0,4},{4,8},{8,12},{12,16},{16,20},{20,24},{24,28},{1,5},{5,9},{9,... | collective-permute-start | bytes 1244168 | tf_op jit(solution)/shard_map/ppermute | solution.py:16
  53.7 1.5 collective-permute-start.1
  55.1 1.3 reshape_squeeze.3
  56.5 1.1 slice_bitcast_fusion.20
  57.6 0.8 copy.54
  58.4 0.7 copy.55
  59.1 0.8 copy.56
  59.9 0.8 copy.57
  60.6 0.8 copy.58
  61.4 0.9 reshape.242
  62.3 10.6 %collective-permute-done = bf16[72,2,1440]{2,1,0:T(2,128)(2,1)S(1)} collective-permute-done((bf16[72,2,1440]{2,1,0:T(2,128)(2,1)S(1)}, bf16[72,2,1440]{2,1,0:T(2,128)(2,1)S(1)}, u32[]{:S(2)}, u32[]{:S(2)}) %collective-permute-start) | collective-permute-done | bytes 414752 | tf_op jit(solution)/shard_map/ppermute | solution.py:16
  72.9 6.1 %fusion.2 = (bf16[72,6,1442]{2,1,0:T(8,128)(2,1)S(1)}, bf16[72,6,1442]{2,1,0:T(8,128)(2,1)S(1)}) fusion(bf16[72,2,1440]{2,1,0:T(2,128)(2,1)S(1)} %collective-permute-done.1, bf16[72,2,1440]{2,1,0:T(2,128)(2,1)S(1)} %multiply_convert_fusion.1, bf16[72,2,1440]{2,1,0:T(2,128)(2,1)S(1)} %collective-permute-done), kind=kLoop, calls=%fused_computation.10 | loop fusion | flops 14950656 | bytes 3735936 | tf_op jit(solution)/shard_map/concatenate | solution.py:70
  79.1 1.6 fusion.12
  80.7 5.2 %fusion.11 = (bf16[5,72,2,1440]{3,2,1,0:T(2,128)(2,1)S(1)}, bf16[5,72,2,1440]{3,2,1,0:T(2,128)(2,1)S(1)}, bf16[5,72,2,1440]{3,2,1,0:T(2,128)(2,1)S(1)}, bf16[5,7...) fusion(bf16[5,72,2,1440]{3,2,1,0:T(2,128)(2,1)S(1)} %get-tuple-element.25, ...), kind=kLoop, calls=%fused_computation.38 | loop fusion | bytes 4423680
  86.3 2.6 bitcast_dynamic-update-slice_fusion
  88.9 5.2 %fusion.10 = (bf16[5,72,2,1440]{3,2,1,0:T(2,128)(2,1)S(1)}, bf16[5,72,2,1440]{3,2,1,0:T(2,128)(2,1)S(1)}, bf16[5,72,2,1440]{3,2,1,0:T(2,128)(2,1)S(1)}, bf16[5,7...) fusion(bf16[5,72,2,1440]{3,2,1,0:T(2,128)(2,1)S(1)} %get-tuple-element.39, ...), kind=kLoop, calls=%fused_computation.36 | loop fusion | bytes 4423680
  94.1 5.4 %fusion.9 = (bf16[5,72,2,1440]{3,2,1,0:T(2,128)(2,1)S(1)}, bf16[5,72,2,1440]{3,2,1,0:T(2,128)(2,1)S(1)}, bf16[5,72,2,1440]{3,2,1,0:T(2,128)(2,1)S(1)}, bf16[5,72...) fusion(bf16[5,72,2,1440]{3,2,1,0:T(2,128)(2,1)S(1)} %get-tuple-element.15, ...), kind=kLoop, calls=%fused_computation.34 | loop fusion | bytes 4423680 | tf_op jit(solution)/shard_map/stack | solution.py:76
  99.5 1.4 copy-done.12
  100.8 1.4 copy-done.13
  102.2 1.4 copy-done.14
  103.6 1.4 copy-done.15
  105.0 1.4 copy-done.16
  106.4 5.4 %reshape.238 = bf16[360,2880]{1,0:T(8,128)(2,1)S(1)} reshape(bf16[5,72,2,1440]{3,2,1,0:T(2,128)(2,1)} %copy-done.16) | data formatting | bytes 4147200 | tf_op jit(solution)/shard_map/reshape | solution.py:78
  111.8 0.8 convolution_bitcast_fusion.4
  112.6 0.8 copy.59
  113.4 0.9 constant_dynamic-update-slice_fusion.4
  114.3 6.3 %reshape.240 = bf16[360,2880]{1,0:T(8,128)(2,1)} reshape(bf16[5,72,2,1440]{3,2,1,0:T(2,128)(2,1)} %copy-done.15) | data formatting | bytes 4147200 | tf_op jit(solution)/shard_map/reshape | solution.py:78
  120.6 3.0 %convolution_bitcast_fusion.3 = f32[72,360]{1,0:T(8,128)} fusion(bf16[360,2880]{1,0:T(8,128)(2,1)} %reshape.240, bf16[72,2880]{1,0:T(8,128)(2,1)S(1)} %reshape_squeeze.3), kind=kOutput, calls=%fused_computation.18 | convolution fusion | flops 149299200 | bytes 2592000 | tf_op jit(solution)/shard_map/dot_general | solution.py:83
  123.6 1.7 copy.60
  125.3 5.4 %reshape.243 = bf16[360,2880]{1,0:T(8,128)(2,1)S(1)} reshape(bf16[5,72,2,1440]{3,2,1,0:T(2,128)(2,1)} %copy-done.14) | data formatting | bytes 4147200 | tf_op jit(solution)/shard_map/reshape | solution.py:78
  130.7 1.4 convolution_bitcast_fusion.2
  132.1 1.7 copy.61
  133.8 5.4 %reshape.245 = bf16[360,2880]{1,0:T(8,128)(2,1)S(1)} reshape(bf16[5,72,2,1440]{3,2,1,0:T(2,128)(2,1)} %copy-done.13) | data formatting | bytes 4147200 | tf_op jit(solution)/shard_map/reshape | solution.py:78
  139.2 1.4 convolution_bitcast_fusion.1
  140.6 1.7 copy.62
  142.3 6.2 %reshape.247 = bf16[360,2880]{1,0:T(8,128)(2,1)} reshape(bf16[5,72,2,1440]{3,2,1,0:T(2,128)(2,1)} %copy-done.12) | data formatting | bytes 4147200 | tf_op jit(solution)/shard_map/reshape | solution.py:78
  148.5 3.0 %convolution_bitcast_fusion = f32[72,360]{1,0:T(8,128)} fusion(bf16[360,2880]{1,0:T(8,128)(2,1)} %reshape.247, bf16[72,2880]{1,0:T(8,128)(2,1)S(1)} %reshape_squeeze.3), kind=kOutput, calls=%fused_computation.15 | convolution fusion | flops 149299200 | bytes 2592000 | tf_op jit(solution)/shard_map/dot_general | solution.py:83
  151.5 1.0 copy.63
  152.6 0.9 constant_dynamic-update-slice_fusion.3
  153.5 0.9 constant_dynamic-update-slice_fusion.2
  154.5 0.9 constant_dynamic-update-slice_fusion.1
  155.5 0.9 copy-done.17
  156.7 2.3 fusion.38
  159.1 0.5 convolution_add_fusion.3
  159.6 1.0 copy-done.4
  161.2 31.9 %all-reduce.3.cloned.1.call-done = f32[5,5,72,72]{2,3,1,0:T(8,128)} async-done(((f32[5,5,72,72]{2,3,1,0:T(8,128)}), f32[5,5,72,72]{2,3,1,0:T(8,128)}) %all-reduce.3.cloned.1.call-update) | async-done | bytes 518416 | tf_op jit(solution)/shard_map/psum | solution.py:93
  193.9 0.8 copy-done
  195.2 1.3 reshape.249
  196.5 77.4 %all-reduce.5.cloned.1.call-done = f32[5,5,72,72]{2,3,1,0:T(8,128)} async-done(((f32[5,5,72,72]{2,3,1,0:T(8,128)}), f32[5,5,72,72]{2,3,1,0:T(8,128)}) %all-reduce.5.cloned.1.call-update) | async-done | bytes 518416 | tf_op jit(solution)/shard_map/psum | solution.py:93
  273.9 1.3 broadcast_multiply_fusion
  275.2 1.2 copy.64
  (64 shorter events, 5.7 us)
Async XLA Ops:
  7.2 3.3 %copy-start.11 = (bf16[1,72,2,1440]{3,2,1,0:T(2,128)(2,1)S(1)}, bf16[1,72,2,1440]{3,2,1,0:T(2,128)(2,1)}, u32[]{:S(2)}) copy-start(bf16[1,72,2,1440]{3,2,1,0:T(2,128)(2,1)} %param.5) | copy-start | bytes 1244164
  7.2 3.6 %copy-start.23 = (f32[72,720]{1,0:T(8,128)S(1)}, f32[72,720]{1,0:T(8,128)}, u32[]{:S(2)}) copy-start(f32[72,720]{1,0:T(8,128)} %param.6) | copy-start | bytes 622084
  7.2 26.4 %all-gather.3.cloned.1.call-start = ((), (), s32[]{:S(2)}) async-start(), calls=%async_computation | async-start | bytes 2211840 | tf_op jit(solution)/shard_map/all_gather | solution.py:63
  9.1 183.9 %all-reduce.3.cloned.1.call-start = ((), (), s32[]{:S(2)}) async-start(), calls=%async_computation.1 | async-start | bytes 1843200 | tf_op jit(solution)/shard_map/psum | solution.py:93
  10.5 13.8 %copy-start.7 = (f32[72,2880]{1,0:T(8,128)}, f32[72,2880]{1,0:T(8,128)S(1)}, u32[]{:S(2)}) copy-start(f32[72,2880]{1,0:T(8,128)S(1)} %reshape.255) | copy-start | bytes 2488324
  10.8 13.3 %copy-start.5 = (f32[1,72,2880]{2,1,0:T(8,128)}, f32[1,72,2880]{2,1,0:T(8,128)S(1)}, u32[]{:S(2)}) copy-start(f32[1,72,2880]{2,1,0:T(8,128)S(1)} %reshape.256) | copy-start | bytes 2488324
  10.8 13.3 %copy-start.24 = (f32[72]{0:T(128)S(1)}, f32[72]{0:T(128)}, u32[]{:S(2)}) copy-start(f32[72]{0:T(128)} %param.7) | copy-start | bytes 868
  22.5 11.1 %copy-start.9 = (f32[2880,72]{0,1:T(8,128)}, f32[2880,72]{0,1:T(8,128)S(1)}, u32[]{:S(2)}) copy-start(f32[2880,72]{0,1:T(8,128)S(1)} %reshape.258) | copy-start | bytes 2488324
  46.9 1.2 copy-start.6
  46.9 1.4 copy-start.8
  46.9 1.6 copy-start.10
  50.3 22.7 %collective-permute-start = (bf16[72,2,1440]{2,1,0:T(2,128)(2,1)S(1)}, bf16[72,2,1440]{2,1,0:T(2,128)(2,1)S(1)}, u32[]{:S(2)}, u32[]{:S(2)}) collective-permute-start(bf16[72,2,1440]{2,1,0:T(2,128)(2,1)S(1)} %multiply_convert_fusion.1), channel_id=1, source_target_pairs={{0,4},{4,8},{8,12},{12,16},{16,20},{20,24},{24,28},{1,5},{5,9},{9,... | collective-permute-start | bytes 1244168 | tf_op jit(solution)/shard_map/ppermute | solution.py:16
  53.7 19.3 %collective-permute-start.1 = (bf16[72,2,1440]{2,1,0:T(2,128)(2,1)S(1)}, bf16[72,2,1440]{2,1,0:T(2,128)(2,1)S(1)}, u32[]{:S(2)}, u32[]{:S(2)}) collective-permute-start(bf16[72,2,1440]{2,1,0:T(2,128)(2,1)S(1)} %multiply_convert_fusion.1), channel_id=1, source_target_pairs={{4,0},{8,4},{12,8},{16,12},{20,16},{24,20},{28,24},{5,1},{9,5},{13... | collective-permute-start | bytes 1244168 | tf_op jit(solution)/shard_map/ppermute | solution.py:17
  99.5 1.4 copy-start.12
  100.8 1.4 copy-start.13
  102.2 1.4 copy-start.14
  103.6 1.4 copy-start.15
  105.0 1.4 copy-start.16
  111.8 8.8 %copy-start.1 = (bf16[360,2880]{1,0:T(8,128)(2,1)}, bf16[360,2880]{1,0:T(8,128)(2,1)S(1)}, u32[]{:S(2)}) copy-start(bf16[360,2880]{1,0:T(8,128)(2,1)S(1)} %reshape.238) | copy-start | bytes 6220804
  130.7 3.1 %copy-start.3 = (bf16[360,2880]{1,0:T(8,128)(2,1)}, bf16[360,2880]{1,0:T(8,128)(2,1)S(1)}, u32[]{:S(2)}) copy-start(bf16[360,2880]{1,0:T(8,128)(2,1)S(1)} %reshape.243) | copy-start | bytes 6220804
  151.5 5.2 %copy-start.22 = (bf16[72,5,72]{0,2,1:T(8,128)(2,1)S(1)}, bf16[72,5,72]{0,2,1:T(8,128)(2,1)}, u32[]{:S(2)}) copy-start(bf16[72,5,72]{0,2,1:T(8,128)(2,1)} %copy.54) | copy-start | bytes 155524
  155.4 3.6 %copy-start.21 = (bf16[72,5,72]{0,2,1:T(8,128)(2,1)S(1)}, bf16[72,5,72]{0,2,1:T(8,128)(2,1)}, u32[]{:S(2)}) copy-start(bf16[72,5,72]{0,2,1:T(8,128)(2,1)} %copy.55) | copy-start | bytes 155524
  155.4 0.9 copy-start.17
  156.4 117.5 %all-reduce.5.cloned.1.call-start = ((), (), s32[]{:S(2)}) async-start(), calls=%async_computation.2 | async-start | bytes 1843200 | tf_op jit(solution)/shard_map/psum | solution.py:93
  156.7 2.3 copy-start.2
  159.0 1.6 copy-start.4
  159.0 1.6 copy-start.20
  160.6 32.4 %copy-start.19 = (bf16[72,5,72]{0,2,1:T(8,128)(2,1)S(1)}, bf16[72,5,72]{0,2,1:T(8,128)(2,1)}, u32[]{:S(2)}) copy-start(bf16[72,5,72]{0,2,1:T(8,128)(2,1)} %copy.57) | copy-start | bytes 155524
  193.0 0.9 copy-start.18
  193.0 1.6 copy-start
Sparse Core Ops, SparseCore 0:
  10.1 23.4 all-gather.2
  156.5 36.4 all-reduce.2
  196.5 77.3 all-reduce.4
